TPU v7x, 768 devices: a whole 4x8x12 slice. The times are simulated.
768 devices in a mesh: seg: 96 (over z, y_lo, core), sub: 8 (over x, y_hi).
Axes of the slice: x: 4, y: 8 (y_hi: 2, y_lo: 4; y = y_hi * 4 + y_lo), z: 12, core: 2. Of those that a mesh axis runs over, the one named last changes fastest.
Arguments:
- state: bfloat16 [4, 128, 1572864], P(None, None, ('seg', 'sub')), may hold values from -6 to 6
- sun_frac: bfloat16 [1572864], P(('seg', 'sub')), may hold values from 0.049804688 to 0.94921875
- land_count: int32 [768], replicated, may hold values from 0 to 2048, as said below
- mixing: bfloat16 [512, 512], replicated, may hold values from -0.25 to 0.25
- canopy_sun: bfloat16 [128, 128], replicated, may hold values from -0.5 to 0.5
- canopy_shade: bfloat16 [128, 128], replicated, may hold values from -0.5 to 0.5
- bias_sun: float32 [128], replicated, may hold values from -3 to 3
- bias_shade: float32 [128], replicated, may hold values from -3 to 3
Outputs:
- tendency: bfloat16 [4, 128, 1572864], P(None, None, ('seg', 'sub'))
Inputs may be any that keep to these rules, and one draw needn't show every extreme that they name: `land_count`: land columns come first in each group.
All inputs are finite; a program needn't handle non-finite values.
Results may differ from a plain program's by a relative error of at most 0.0035.
Values may be sent and summed in bfloat16 or wider, within the bound.
No kernel may reach another device: no remote copies, remote signals or barrier semaphores. Data moves between devices by JAX's collectives and lax.ppermute only.
A program may use at most 32 MiB of HBM per device.

v0:
```python
import jax
import jax.numpy as jnp
from jax import lax
from jax.experimental import pallas as pl
from jax.experimental.pallas import tpu as pltpu
from jax.sharding import PartitionSpec as P

FIELDS = 4
LEV = 128
CANLEV = 32
ITERS = 4
EDGE = 128
ROWS = FIELDS * LEV
BLOCK = 256
AXES = ("seg", "sub")


def canopy_rows(values):
    return jnp.concatenate(
        [values[f * LEV + LEV - CANLEV : (f + 1) * LEV] for f in range(FIELDS)], axis=0
    )


def physics(cols, frac, land, mixing, pair, bias):
    raw = jnp.dot(mixing, cols, preferred_element_type=jnp.float32)
    rounded = canopy_rows(cols)
    low = rounded.astype(jnp.float32)
    half = low.shape[0]
    of_sun = 0.5 * frac
    of_shade = 0.5 - of_sun
    current = low
    for step in range(ITERS):
        if step:
            rounded = current.astype(jnp.bfloat16)
        drive = jnp.tanh(jnp.dot(pair, rounded, preferred_element_type=jnp.float32) + bias)
        current = current + (of_sun * drive[:half] + of_shade * drive[half:])
    added = jnp.where(land, current - low, 0.0).astype(jnp.bfloat16).astype(jnp.float32)
    parts = []
    for f in range(FIELDS):
        top = f * LEV + LEV - CANLEV
        parts.append(raw[f * LEV : top])
        parts.append(raw[top : (f + 1) * LEV] + added[f * CANLEV : (f + 1) * CANLEV])
    return jnp.concatenate(parts, axis=0)


def parameters(mixing_ref, sun_ref, shade_ref, bias_sun_ref, bias_shade_ref, count):
    pair = jnp.concatenate([sun_ref[...], shade_ref[...]], axis=0)
    rows = sun_ref.shape[0]
    bias = jnp.concatenate(
        [
            jnp.broadcast_to(bias_sun_ref[...], (rows, rows)).T,
            jnp.broadcast_to(bias_shade_ref[...], (rows, rows)).T,
        ],
        axis=0,
    )
    return mixing_ref[...], pair, jnp.concatenate([bias] * (count // rows), axis=1)


def group_here(offset):
    nsub = lax.axis_size("sub")
    groups = nsub * lax.axis_size("seg")
    return (lax.axis_index("seg") * nsub + lax.axis_index("sub") + groups + offset) % groups


def own_kernel(land_ref, cols_ref, frac_ref, mixing_ref, sun_ref, shade_ref, bs_ref, bh_ref, out_ref, first_ref, last_ref):
    step = pl.program_id(0)
    width = cols_ref.shape[1]
    params = parameters(mixing_ref, sun_ref, shade_ref, bs_ref, bh_ref, width)
    count = land_ref[group_here(0)]
    land = step * width + lax.broadcasted_iota(jnp.int32, (1, width), 1) < count
    raw = physics(cols_ref[...], frac_ref[...].astype(jnp.float32), land, *params)
    out_ref[...] = raw.astype(jnp.bfloat16)

    @pl.when(step == 0)
    def _():
        first_ref[...] = raw[:, :EDGE]

    @pl.when(step == pl.num_programs(0) - 1)
    def _():
        last_ref[...] = raw[:, width - EDGE :]


def edge_kernel(offset, start, land_ref, got_ref, own_ref, mixing_ref, sun_ref, shade_ref, bs_ref, bh_ref, all_ref, out_ref):
    del all_ref
    params = parameters(mixing_ref, sun_ref, shade_ref, bs_ref, bh_ref, EDGE)
    count = land_ref[group_here(offset)]
    land = start + lax.broadcasted_iota(jnp.int32, (1, EDGE), 1) < count
    frac = got_ref[ROWS : ROWS + 1, :].astype(jnp.float32)
    raw = physics(got_ref[:ROWS, :], frac, land, *params)
    out_ref[...] = (own_ref[...] + raw).astype(jnp.bfloat16)


def whole(shape):
    return pl.BlockSpec(shape, lambda *_: (0,) * len(shape))


def per_device(state, sun_frac, land_count, mixing, canopy_sun, canopy_shade, bias_sun, bias_shade):
    width = state.shape[2]
    half = FIELDS * CANLEV
    cols = state.reshape(ROWS, width)
    groups = lax.axis_size(AXES)
    up = [(i, (i + 1) % groups) for i in range(groups)]
    down = [(b, a) for a, b in up]

    def packed(start):
        edge = lax.slice_in_dim(cols, start, start + EDGE, axis=1)
        share = lax.slice_in_dim(sun_frac, start, start + EDGE, axis=0)
        return jnp.concatenate([edge, jnp.broadcast_to(share[None, :], (16, EDGE))], axis=0)

    from_left = lax.ppermute(packed(width - EDGE), AXES, up)
    from_right = lax.ppermute(packed(0), AXES, down)
    params = (mixing, canopy_sun, canopy_shade, bias_sun.reshape(1, half), bias_shade.reshape(1, half))
    param_specs = [whole((ROWS, ROWS)), whole((half, half)), whole((half, half)), whole((1, half)), whole((1, half))]
    steps = width // BLOCK
    out, first, last = pl.pallas_call(
        own_kernel,
        out_shape=(
            jax.ShapeDtypeStruct((ROWS, width), jnp.bfloat16),
            jax.ShapeDtypeStruct((ROWS, EDGE), jnp.float32),
            jax.ShapeDtypeStruct((ROWS, EDGE), jnp.float32),
        ),
        grid_spec=pltpu.PrefetchScalarGridSpec(
            num_scalar_prefetch=1,
            grid=(steps,),
            in_specs=[
                pl.BlockSpec((ROWS, BLOCK), lambda i, *_: (0, i)),
                pl.BlockSpec((1, BLOCK), lambda i, *_: (0, i)),
                *param_specs,
            ],
            out_specs=[
                pl.BlockSpec((ROWS, BLOCK), lambda i, *_: (0, i)),
                whole((ROWS, EDGE)),
                whole((ROWS, EDGE)),
            ],
        ),
        compiler_params=pltpu.CompilerParams(dimension_semantics=("arbitrary",)),
        name="own_columns",
    )(land_count, cols, sun_frac.reshape(1, width), *params)

    def with_edge(out, got, own, offset, start, block, name):
        def body(*refs):
            edge_kernel(offset, start, *refs)

        return pl.pallas_call(
            body,
            out_shape=jax.ShapeDtypeStruct((ROWS, width), jnp.bfloat16),
            grid_spec=pltpu.PrefetchScalarGridSpec(
                num_scalar_prefetch=1,
                grid=(1,),
                in_specs=[
                    whole(got.shape),
                    whole((ROWS, EDGE)),
                    *param_specs,
                    pl.BlockSpec(memory_space=pl.ANY),
                ],
                out_specs=pl.BlockSpec((ROWS, EDGE), lambda i, *_: (0, block)),
            ),
            input_output_aliases={8: 0},
            compiler_params=pltpu.CompilerParams(dimension_semantics=("arbitrary",)),
            name=name,
        )(land_count, got, own, *params, out)

    out = with_edge(out, from_left, first, -1, width - EDGE, 0, "left_edge")
    out = with_edge(out, from_right, last, 1, 0, width // EDGE - 1, "right_edge")
    return out.reshape(state.shape)


def solution(mesh):
    in_specs = (P(None, None, AXES), P(AXES), P(), P(), P(), P(), P(), P())
    out_specs = P(None, None, AXES)
    return jax.shard_map(
        per_device, mesh=mesh, in_specs=in_specs, out_specs=out_specs, check_vma=False
    )
```

profile of v0, /device:TPU:1, one launch (start us, length us, event | category | flops | bytes accessed | tf_op | source)
XLA Modules:
  0.0 34.4 jit_solution(9709054739706777092)
XLA Ops:
  0.0 1.0 %fusion = (bf16[512,128]{1,0:T(8,128)(2,1)S(1)}, bf16[512,128]{1,0:T(8,128)(2,1)S(1)}) fusion(bf16[512,2048]{1,0:T(8,128)(2,1)} %bitcast.4), kind=kLoop, calls=%fused_computation.2 | loop fusion | bytes 524288 | tf_op jit(solution)/shard_map/slice | solution.py:106
  1.0 0.7 %fusion.1 = (bf16[128]{0:T(256)(128)(2,1)S(1)}, bf16[128]{0:T(256)(128)(2,1)S(1)}) fusion(bf16[2048]{0:T(1024)(128)(2,1)} %param.9), kind=kLoop, calls=%fused_computation.3 | loop fusion | bytes 1024 | tf_op jit(solution)/shard_map/slice | solution.py:107
  1.7 8.3 %collective-permute-start.1 = (bf16[528,128]{1,0:T(8,128)(2,1)S(1)}, bf16[528,128]{1,0:T(8,128)(2,1)S(1)}, u32[]{:S(2)}, u32[]{:S(2)}) collective-permute-start(bf16[528,128]{1,0:T(8,128)(2,1)S(1)} %pad_maximum_fusion.1), channel_id=1, source_target_pairs={{0,1},{1,2},{2,3},{3,4},{4,5},{5,6},{6,7},{7,8},{8,9},{9,10},{10,1... | collective-permute-start | bytes 405512 | tf_op jit(solution)/shard_map/ppermute | solution.py:110
  10.0 4.7 %collective-permute-start = (bf16[528,128]{1,0:T(8,128)(2,1)S(1)}, bf16[528,128]{1,0:T(8,128)(2,1)S(1)}, u32[]{:S(2)}, u32[]{:S(2)}) collective-permute-start(bf16[528,128]{1,0:T(8,128)(2,1)S(1)} %pad_maximum_fusion), channel_id=1, source_target_pairs={{1,0},{2,1},{3,2},{4,3},{5,4},{6,5},{7,6},{8,7},{9,8},{10,9},{11,1... | collective-permute-start | bytes 405512 | tf_op jit(solution)/shard_map/ppermute | solution.py:111
  14.7 1.3 %reshape.18.frac_ref = bf16[1,2048]{1,0:T(2,128)(2,1)} reshape(bf16[2048]{0:T(1024)(128)(2,1)} %param.9) | data formatting | bytes 8192 | tf_op jit(solution)/shard_map/reshape | solution.py:138
  16.0 10.2 %own_columns.1 = (bf16[512,2048]{1,0:T(8,128)(2,1)}, f32[512,128]{1,0:T(8,128)}, f32[512,128]{1,0:T(8,128)}) custom-call(s32[768]{0:T(1024)} %refs_0_.3, bf16[512,2048]{1,0:T(8,128)(2,1)} %bitcast.5, bf16[1,2048]{1,0:T(2,128)(2,1)} %reshape.18.frac_ref, bf16[512,512]{1,0:T(8,128)(2,1)} %refs_3_.3, bf16[128,128]{1,0:T(8,128)(2,1)} %refs_4_.3, ...), custom_call_target="tpu_custom_call" | custom-call | tf_op jit(solution)/shard_map/own_columns/pallas_call | solution.py:115
  26.2 0.0 collective-permute-done.1.refs_1_
  26.2 0.0 copy-start
  26.2 0.6 %copy-done = bf16[528,128]{1,0:T(8,128)(2,1)} copy-done((bf16[528,128]{1,0:T(8,128)(2,1)}, bf16[528,128]{1,0:T(8,128)(2,1)S(1)}, u32[]{:S(2)}) %copy-start) | copy-done | bytes 135192
  26.9 3.4 %left_edge.1.refs_8_ = bf16[512,2048]{1,0:T(8,128)(2,1)} custom-call(s32[768]{0:T(1024)} %refs_0_.3, bf16[528,128]{1,0:T(8,128)(2,1)} %copy-done, f32[512,128]{1,0:T(8,128)} %get-tuple-element.9.refs_2_, bf16[512,512]{1,0:T(8,128)(2,1)} %refs_3_.3, bf16[128,128]{1,0:T(8,128)(2,1)} %refs_4_.3, ...), custom_call_target="tpu_custom_call", output_to_operand_aliasing={{}: (8, {})} | custom-call | tf_op jit(solution)/shard_map/left_edge/pallas_call | solution.py:144
  30.3 0.0 collective-permute-done.refs_1_
  30.3 0.0 copy-start.1
  30.3 0.6 %copy-done.1 = bf16[528,128]{1,0:T(8,128)(2,1)} copy-done((bf16[528,128]{1,0:T(8,128)(2,1)}, bf16[528,128]{1,0:T(8,128)(2,1)S(1)}, u32[]{:S(2)}) %copy-start.1) | copy-done | bytes 135192
  30.9 3.4 %right_edge.1 = bf16[512,2048]{1,0:T(8,128)(2,1)} custom-call(s32[768]{0:T(1024)} %refs_0_.3, bf16[528,128]{1,0:T(8,128)(2,1)} %copy-done.1, f32[512,128]{1,0:T(8,128)} %get-tuple-element.8.refs_2_, bf16[512,512]{1,0:T(8,128)(2,1)} %refs_3_.3, bf16[128,128]{1,0:T(8,128)(2,1)} %refs_4_.3, bf16[128,128]{1,0:T(8,128)(2,1)} %refs_5_.3, ...), custom_call_target="tpu_custom_call", output_to_operand_aliasing={{}: (8, {})} | custom-call | tf_op jit(solution)/shard_map/right_edge/pallas_call | solution.py:144
  (4 shorter events, 0.0 us)
Async XLA Ops:
  1.7 24.5 %collective-permute-start.1 = (bf16[528,128]{1,0:T(8,128)(2,1)S(1)}, bf16[528,128]{1,0:T(8,128)(2,1)S(1)}, u32[]{:S(2)}, u32[]{:S(2)}) collective-permute-start(bf16[528,128]{1,0:T(8,128)(2,1)S(1)} %pad_maximum_fusion.1), channel_id=1, source_target_pairs={{0,1},{1,2},{2,3},{3,4},{4,5},{5,6},{6,7},{7,8},{8,9},{9,10},{10,1... | collective-permute-start | bytes 405512 | tf_op jit(solution)/shard_map/ppermute | solution.py:110
  10.0 20.3 %collective-permute-start = (bf16[528,128]{1,0:T(8,128)(2,1)S(1)}, bf16[528,128]{1,0:T(8,128)(2,1)S(1)}, u32[]{:S(2)}, u32[]{:S(2)}) collective-permute-start(bf16[528,128]{1,0:T(8,128)(2,1)S(1)} %pad_maximum_fusion), channel_id=1, source_target_pairs={{1,0},{2,1},{3,2},{4,3},{5,4},{6,5},{7,6},{8,7},{9,8},{10,9},{11,1... | collective-permute-start | bytes 405512 | tf_op jit(solution)/shard_map/ppermute | solution.py:111
  26.2 0.6 %copy-start = (bf16[528,128]{1,0:T(8,128)(2,1)}, bf16[528,128]{1,0:T(8,128)(2,1)S(1)}, u32[]{:S(2)}) copy-start(bf16[528,128]{1,0:T(8,128)(2,1)S(1)} %collective-permute-done.1.refs_1_) | copy-start | bytes 405508
  30.3 0.7 %copy-start.1 = (bf16[528,128]{1,0:T(8,128)(2,1)}, bf16[528,128]{1,0:T(8,128)(2,1)S(1)}, u32[]{:S(2)}) copy-start(bf16[528,128]{1,0:T(8,128)(2,1)S(1)} %collective-permute-done.refs_1_) | copy-start | bytes 405508
where the time goes:
time: 34.9 us; the launch traced here: 34.4 us
  Pallas kernels  17.1 us (49%)
  starting transfers between devices  12.9 us (37%)
  local copies, waits for them, and re-layouts  4.28 us (12%)
    pallas_call x1, Pallas kernels, per_device(): pl.pallas_call(own_kernel, out_shape=(jax.ShapeDtypeStruct((ROWS, width),...  10.2 us
    ppermute x1, starting transfers between devices, per_device(): from_left = lax.ppermute(packed(width - EDGE), AXES, up)  8.27 us
    pallas_call x2, Pallas kernels, with_edge(): pl.pallas_call(body, out_shape=jax.ShapeDtypeStruct((ROWS, width), jnp.bf...  6.86 us
    ppermute x1, starting transfers between devices, per_device(): from_right = lax.ppermute(packed(0), AXES, down)  4.68 us
    reshape x1, local copies, waits for them, and re-layouts, per_device(): sun_frac.reshape(1, width)  1.29 us
    unnamed x4, local copies, waits for them, and re-layouts  1.29 us
    slice x1, local copies, waits for them, and re-layouts, packed(): edge = lax.slice_in_dim(cols, start, start + EDGE, axis=1)  0.99 us
    slice x1, local copies, waits for them, and re-layouts, packed(): share = lax.slice_in_dim(sun_frac, start, start + EDGE, axis=0)  0.71 us
  transfers between devices with their start and end apart: 2, of which 0 were waited for; matrix products, arithmetic and copies ran while one was open for 4% of the time, Pallas kernels for 40%

commit v1 on v0

v1 whole, which is shorter than its diff:
```python
import jax
import jax.numpy as jnp
from jax import lax
from jax.experimental import pallas as pl
from jax.experimental.pallas import tpu as pltpu
from jax.sharding import PartitionSpec as P

FIELDS = 4
LEV = 128
CANLEV = 32
ITERS = 4
EDGE = 128
ROWS = FIELDS * LEV
HALF = FIELDS * CANLEV
CHUNK = 256
VMEM_BYTES = 16 * 2**20
AXES = ("seg", "sub")
F32 = jnp.float32
BF16 = jnp.bfloat16


def canopy_rows(values):
    return jnp.concatenate(
        [values[f * LEV + LEV - CANLEV : (f + 1) * LEV] for f in range(FIELDS)], axis=0
    )


def physics(cols, frac, land, mixing, pair, bias):
    raw = jnp.dot(mixing, cols, preferred_element_type=F32)
    rounded = canopy_rows(cols)
    low = rounded.astype(F32)
    of_sun = 0.5 * frac
    of_shade = 0.5 - of_sun
    current = low
    for step in range(ITERS):
        if step:
            rounded = current.astype(BF16)
        drive = jnp.tanh(jnp.dot(pair, rounded, preferred_element_type=F32) + bias)
        current = current + (of_sun * drive[:HALF] + of_shade * drive[HALF:])
    added = jnp.where(land, current - low, 0.0).astype(BF16).astype(F32)
    parts = []
    for f in range(FIELDS):
        top = f * LEV + LEV - CANLEV
        parts.append(raw[f * LEV : top])
        parts.append(raw[top : (f + 1) * LEV] + added[f * CANLEV : (f + 1) * CANLEV])
    return jnp.concatenate(parts, axis=0)


def group_here():
    return lax.axis_index("seg") * lax.axis_size("sub") + lax.axis_index("sub")


def lanes():
    return lax.broadcasted_iota(jnp.int32, (1, EDGE), 1)


def edges_kernel(
    land_ref, cols_ref, frac_ref, mixing_ref, sun_ref, shade_ref, bias_sun_ref, bias_shade_ref,
    send_first, send_last, raw_first, raw_last, mixing_out, pair_out, bias_out, frac_out, land_out, inner_out,
    cols_buf, frac_buf, bias_buf, land_buf, sems,
):
    width = cols_ref.shape[1]
    moves = [
        (cols_ref.at[:, pl.ds(0, EDGE)], cols_buf.at[:, pl.ds(0, EDGE)]),
        (cols_ref.at[:, pl.ds(width - EDGE, EDGE)], cols_buf.at[:, pl.ds(EDGE, EDGE)]),
        (sun_ref, pair_out.at[pl.ds(0, HALF)]),
        (shade_ref, pair_out.at[pl.ds(HALF, HALF)]),
        (frac_ref, frac_buf),
        (bias_sun_ref, bias_buf.at[pl.ds(0, 1)]),
        (bias_shade_ref, bias_buf.at[pl.ds(1, 1)]),
        (land_ref, land_buf),
        (mixing_ref, mixing_out),
        (cols_ref.at[:, pl.ds(EDGE, width - 2 * EDGE)], inner_out),
    ]
    copies = [pltpu.make_async_copy(a, b, sems.at[i]) for i, (a, b) in enumerate(moves)]
    for copy in copies:
        copy.start()
    for copy in copies[:-1]:
        copy.wait()
    bias = jnp.concatenate(
        [jnp.broadcast_to(bias_buf[i : i + 1, :], (HALF, HALF)).T for i in range(2)], axis=0
    )
    bias_out[...] = bias
    frac = frac_buf[...].astype(F32)
    frac_out[...] = frac
    count = land_buf[group_here()]
    column = lax.broadcasted_iota(jnp.int32, frac.shape, 0) * EDGE + lax.broadcasted_iota(jnp.int32, frac.shape, 1)
    land_out[...] = (column < count).astype(F32)
    land = jnp.concatenate([lanes(), lanes() + (width - EDGE)], axis=1) < count
    ends = jnp.concatenate([frac[:1], frac[frac.shape[0] - 1 :]], axis=1)
    raw = physics(
        cols_buf[...], ends, land, mixing_out[...], pair_out[...], jnp.concatenate([bias, bias], axis=1)
    )
    raw_first[...] = raw[:, :EDGE]
    raw_last[...] = raw[:, EDGE:]
    send_first[...] = raw[:, :EDGE].astype(BF16)
    send_last[...] = raw[:, EDGE:].astype(BF16)
    copies[-1].wait()


def inner_kernel(cols_ref, frac_ref, land_ref, mixing_ref, pair_ref, bias_ref, out_ref, buf, sems):
    bias = jnp.concatenate([bias_ref[...]] * (CHUNK // EDGE), axis=1)
    copies = []
    def spread(ref, row):
        return jnp.concatenate([ref[row + k : row + k + 1, :] for k in range(CHUNK // EDGE)], axis=1)

    for c in range(cols_ref.shape[1] // CHUNK):
        start = EDGE + c * CHUNK
        row = start // EDGE
        frac = spread(frac_ref, row)
        land = spread(land_ref, row) > 0.5
        raw = physics(cols_ref[:, c * CHUNK : (c + 1) * CHUNK], frac, land, mixing_ref[...], pair_ref[...], bias)
        buf[c] = raw.astype(BF16)
        copies.append(pltpu.make_async_copy(buf.at[c], out_ref.at[:, pl.ds(start, CHUNK)], sems.at[c]))
        copies[-1].start()
    for copy in copies:
        copy.wait()


def join_kernel(block, got_ref, own_ref, all_ref, out_ref, buf, sem):
    del all_ref
    buf[...] = (own_ref[...] + got_ref[...].astype(F32)).astype(BF16)
    copy = pltpu.make_async_copy(buf, out_ref.at[:, pl.ds(block * EDGE, EDGE)], sem)
    copy.start()
    copy.wait()


def off_chip(value):
    return pltpu.with_memory_space_constraint(value, pltpu.HBM)


def on_chip(value):
    return pltpu.with_memory_space_constraint(value, pltpu.VMEM)


HBM = pl.BlockSpec(memory_space=pltpu.HBM)
VMEM = pl.BlockSpec(memory_space=pltpu.VMEM)


def per_device(state, sun_frac, land_count, mixing, canopy_sun, canopy_shade, bias_sun, bias_shade):
    width = state.shape[2]
    cols = state.reshape(ROWS, width)
    groups = lax.axis_size(AXES)
    up = [(i, (i + 1) % groups) for i in range(groups)]
    down = [(b, a) for a, b in up]
    frac = sun_frac.reshape(width // EDGE, EDGE)
    chunks = (width - 2 * EDGE) // CHUNK

    send_first, send_last, raw_first, raw_last, mix, pair, bias, frac, land, inner = pl.pallas_call(
        edges_kernel,
        out_shape=(
            pltpu.VMEM((ROWS, EDGE), BF16),
            pltpu.VMEM((ROWS, EDGE), BF16),
            pltpu.VMEM((ROWS, EDGE), F32),
            pltpu.VMEM((ROWS, EDGE), F32),
            pltpu.VMEM((ROWS, ROWS), BF16),
            pltpu.VMEM((2 * HALF, HALF), BF16),
            pltpu.VMEM((2 * HALF, EDGE), F32),
            pltpu.VMEM((width // EDGE, EDGE), F32),
            pltpu.VMEM((width // EDGE, EDGE), F32),
            pltpu.VMEM((ROWS, width - 2 * EDGE), BF16),
        ),
        in_specs=[HBM] * 8,
        out_specs=[VMEM] * 10,
        scratch_shapes=[
            pltpu.VMEM((ROWS, 2 * EDGE), BF16),
            pltpu.VMEM((width // EDGE, EDGE), BF16),
            pltpu.VMEM((2, HALF), F32),
            pltpu.SMEM(land_count.shape, jnp.int32),
            pltpu.SemaphoreType.DMA((10,)),
        ],
        compiler_params=pltpu.CompilerParams(vmem_limit_bytes=VMEM_BYTES),
        name="edges",
    )(*map(off_chip, (land_count, cols, frac, mixing, canopy_sun, canopy_shade, bias_sun.reshape(1, HALF), bias_shade.reshape(1, HALF))))

    from_left = lax.ppermute(send_last, AXES, up)
    from_right = lax.ppermute(send_first, AXES, down)

    out = pl.pallas_call(
        inner_kernel,
        out_shape=jax.ShapeDtypeStruct((ROWS, width), BF16),
        in_specs=[VMEM] * 6,
        out_specs=HBM,
        scratch_shapes=[pltpu.VMEM((chunks, ROWS, CHUNK), BF16), pltpu.SemaphoreType.DMA((chunks,))],
        compiler_params=pltpu.CompilerParams(vmem_limit_bytes=VMEM_BYTES),
        name="inner",
    )(on_chip(inner), on_chip(frac), on_chip(land), on_chip(mix), on_chip(pair), on_chip(bias))

    def joined(out, got, own, block, name):
        def body(*refs):
            join_kernel(block, *refs)

        return pl.pallas_call(
            body,
            out_shape=jax.ShapeDtypeStruct((ROWS, width), BF16),
            in_specs=[VMEM, VMEM, HBM],
            out_specs=HBM,
            scratch_shapes=[pltpu.VMEM((ROWS, EDGE), BF16), pltpu.SemaphoreType.DMA],
            input_output_aliases={2: 0},
            compiler_params=pltpu.CompilerParams(vmem_limit_bytes=VMEM_BYTES),
            name=name,
        )(on_chip(got), on_chip(own), out)

    out = joined(out, from_left, raw_first, 0, "join_left")
    out = joined(out, from_right, raw_last, width // EDGE - 1, "join_right")
    return out.reshape(state.shape)


def solution(mesh):
    in_specs = (P(None, None, AXES), P(AXES), P(), P(), P(), P(), P(), P())
    out_specs = P(None, None, AXES)
    return jax.shard_map(
        per_device, mesh=mesh, in_specs=in_specs, out_specs=out_specs, check_vma=False
    )
```

time: 34.9 us -> 26.9 us (0.77)
  the two profiles are of different devices: /device:TPU:1 before, /device:TPU:384 now
where the time goes in v1:
time: 26.9 us; the launch traced here: 26.7 us
  starting transfers between devices  9.78 us (36%)
  Pallas kernels  8.71 us (32%)
  waiting for transfers between devices  8.17 us (30%)
    ppermute x1, waiting for transfers between devices, per_device(): from_right = lax.ppermute(send_first, AXES, down)  8.17 us
    ppermute x1, starting transfers between devices, per_device(): from_left = lax.ppermute(send_last, AXES, up)  7.74 us
    pallas_call x1, Pallas kernels, per_device(): pl.pallas_call(inner_kernel, out_shape=jax.ShapeDtypeStruct((ROWS, width)...  5.16 us
    pallas_call x1, Pallas kernels, per_device(): pl.pallas_call(edges_kernel, out_shape=(pltpu.VMEM((ROWS, EDGE), BF16), p...  2.17 us
    ppermute x1, starting transfers between devices, per_device(): from_right = lax.ppermute(send_first, AXES, down)  2.04 us
    pallas_call x2, Pallas kernels, joined(): pl.pallas_call(body, out_shape=jax.ShapeDtypeStruct((ROWS, width), BF16),...  1.38 us
  transfers between devices with their start and end apart: 2, of which 1 were waited for; matrix products, arithmetic and copies ran while one was open for 0% of the time, Pallas kernels for 22%

profile of v1, /device:TPU:384, one launch (start us, length us, event | category | flops | bytes accessed | tf_op | source)
XLA Modules:
  0.0 26.7 jit_solution(5512788107357444575)
XLA Ops:
  0.0 2.2 %edges.1 = (bf16[512,128]{1,0:T(8,128)(2,1)S(1)}, bf16[512,128]{1,0:T(8,128)(2,1)S(1)}, f32[512,128]{1,0:T(8,128)S(1)}, f32[512,128]{1,0:T(8,128)S(1)}, bf16[512...) custom-call(s32[768]{0:T(1024)} %land_ref.1, ...), custom_call_target="tpu_custom_call" | custom-call | tf_op jit(solution)/shard_map/edges/pallas_call | solution.py:149
  2.2 7.7 %collective-permute-start.1 = (bf16[512,128]{1,0:T(8,128)(2,1)S(1)}, bf16[512,128]{1,0:T(8,128)(2,1)S(1)}, u32[]{:S(2)}, u32[]{:S(2)}) collective-permute-start(bf16[512,128]{1,0:T(8,128)(2,1)S(1)} %get-tuple-element.17), channel_id=1, source_target_pairs={{0,1},{1,2},{2,3},{3,4},{4,5},{5,6},{6,7},{7,8},{8,9},{9,10},{10,1... | collective-permute-start | bytes 393224 | tf_op jit(solution)/shard_map/ppermute | solution.py:176
  9.9 2.0 %collective-permute-start = (bf16[512,128]{1,0:T(8,128)(2,1)S(1)}, bf16[512,128]{1,0:T(8,128)(2,1)S(1)}, u32[]{:S(2)}, u32[]{:S(2)}) collective-permute-start(bf16[512,128]{1,0:T(8,128)(2,1)S(1)} %get-tuple-element.15), channel_id=1, source_target_pairs={{1,0},{2,1},{3,2},{4,3},{5,4},{6,5},{7,6},{8,7},{9,8},{10,9},{11,1... | collective-permute-start | bytes 393224 | tf_op jit(solution)/shard_map/ppermute | solution.py:177
  12.0 5.2 %inner.1.refs_2_ = bf16[512,2048]{1,0:T(8,128)(2,1)} custom-call(bf16[512,1792]{1,0:T(8,128)(2,1)S(1)} %get-tuple-element.19.cols_ref, f32[16,128]{1,0:T(8,128)S(1)} %get-tuple-element.20.frac_ref, f32[16,128]{1,0:T(8,128)S(1)} %get-tuple-element.21.land_ref, bf16[512,512]{1,0:T(8,128)(2,1)S(1)} %get-tuple-element.22.mixing_ref, ...), custom_call_target="tpu_custom_call" | custom-call | tf_op jit(solution)/shard_map/inner/pallas_call | solution.py:179
  17.1 0.0 collective-permute-done.1.refs_0_
  17.2 0.7 %join_left.1.refs_2_ = bf16[512,2048]{1,0:T(8,128)(2,1)} custom-call(bf16[512,128]{1,0:T(8,128)(2,1)S(1)} %collective-permute-done.1.refs_0_, f32[512,128]{1,0:T(8,128)S(1)} %get-tuple-element.18.refs_1_, bf16[512,2048]{1,0:T(8,128)(2,1)} %inner.1.refs_2_), custom_call_target="tpu_custom_call", output_to_operand_aliasing={{}: (2, {})} | custom-call | tf_op jit(solution)/shard_map/join_left/pallas_call | solution.py:193
  17.9 8.2 %collective-permute-done.refs_0_ = bf16[512,128]{1,0:T(8,128)(2,1)S(1)} collective-permute-done((bf16[512,128]{1,0:T(8,128)(2,1)S(1)}, bf16[512,128]{1,0:T(8,128)(2,1)S(1)}, u32[]{:S(2)}, u32[]{:S(2)}) %collective-permute-start) | collective-permute-done | bytes 131104 | tf_op jit(solution)/shard_map/ppermute | solution.py:177
  26.0 0.7 %join_right.1 = bf16[512,2048]{1,0:T(8,128)(2,1)} custom-call(bf16[512,128]{1,0:T(8,128)(2,1)S(1)} %collective-permute-done.refs_0_, f32[512,128]{1,0:T(8,128)S(1)} %get-tuple-element.16.refs_1_, bf16[512,2048]{1,0:T(8,128)(2,1)} %join_left.1.refs_2_), custom_call_target="tpu_custom_call", output_to_operand_aliasing={{}: (2, {})} | custom-call | tf_op jit(solution)/shard_map/join_right/pallas_call | solution.py:193
Async XLA Ops:
  2.2 15.0 %collective-permute-start.1 = (bf16[512,128]{1,0:T(8,128)(2,1)S(1)}, bf16[512,128]{1,0:T(8,128)(2,1)S(1)}, u32[]{:S(2)}, u32[]{:S(2)}) collective-permute-start(bf16[512,128]{1,0:T(8,128)(2,1)S(1)} %get-tuple-element.17), channel_id=1, source_target_pairs={{0,1},{1,2},{2,3},{3,4},{4,5},{5,6},{6,7},{7,8},{8,9},{9,10},{10,1... | collective-permute-start | bytes 393224 | tf_op jit(solution)/shard_map/ppermute | solution.py:176
  9.9 16.1 %collective-permute-start = (bf16[512,128]{1,0:T(8,128)(2,1)S(1)}, bf16[512,128]{1,0:T(8,128)(2,1)S(1)}, u32[]{:S(2)}, u32[]{:S(2)}) collective-permute-start(bf16[512,128]{1,0:T(8,128)(2,1)S(1)} %get-tuple-element.15), channel_id=1, source_target_pairs={{1,0},{2,1},{3,2},{4,3},{5,4},{6,5},{7,6},{8,7},{9,8},{10,9},{11,1... | collective-permute-start | bytes 393224 | tf_op jit(solution)/shard_map/ppermute | solution.py:177

commit v2 on v1

--- a/solution.py
+++ b/solution.py
@@ -50,13 +50,18 @@
     return lax.axis_index("seg") * lax.axis_size("sub") + lax.axis_index("sub")
 
 
+def relaxed(group):
+    nsub = lax.axis_size("sub")
+    return ((group // nsub) % 8 == 0) & (group >= nsub)
+
+
 def lanes():
     return lax.broadcasted_iota(jnp.int32, (1, EDGE), 1)
 
 
 def edges_kernel(
     land_ref, cols_ref, frac_ref, mixing_ref, sun_ref, shade_ref, bias_sun_ref, bias_shade_ref,
-    send_first, send_last, raw_first, raw_last, mixing_out, pair_out, bias_out, frac_out, land_out, inner_out,
+    send_first, send_last, send_mixed, raw_first, raw_last, mixing_out, pair_out, bias_out, frac_out, land_out, inner_out,
     cols_buf, frac_buf, bias_buf, land_buf, sems,
 ):
     width = cols_ref.shape[1]
@@ -91,10 +96,22 @@
     raw = physics(
         cols_buf[...], ends, land, mixing_out[...], pair_out[...], jnp.concatenate([bias, bias], axis=1)
     )
-    raw_first[...] = raw[:, :EDGE]
-    raw_last[...] = raw[:, EDGE:]
-    send_first[...] = raw[:, :EDGE].astype(BF16)
-    send_last[...] = raw[:, EDGE:].astype(BF16)
+    first, last = raw[:, :EDGE], raw[:, EDGE:]
+    raw_first[...] = first
+    raw_last[...] = last
+    send_first[...] = first.astype(BF16)
+    send_last[...] = last.astype(BF16)
+    group = group_here()
+    early_last = jnp.logical_and(group % 2 == 0, relaxed(group))
+
+    @pl.when(early_last)
+    def _():
+        send_mixed[...] = last.astype(BF16)
+
+    @pl.when(jnp.logical_not(early_last))
+    def _():
+        send_mixed[...] = first.astype(BF16)
+
     copies[-1].wait()
 
 
@@ -117,12 +134,30 @@
         copy.wait()
 
 
-def join_kernel(block, got_ref, own_ref, all_ref, out_ref, buf, sem):
+def join_kernel(got_a, got_b, got_c, first_ref, last_ref, all_ref, out_ref, buf, sems):
     del all_ref
-    buf[...] = (own_ref[...] + got_ref[...].astype(F32)).astype(BF16)
-    copy = pltpu.make_async_copy(buf, out_ref.at[:, pl.ds(block * EDGE, EDGE)], sem)
-    copy.start()
-    copy.wait()
+    group = group_here()
+    groups = lax.axis_size(AXES)
+    odd = group % 2 == 1
+    left_in_b = jnp.logical_and(odd, relaxed(group))
+    right_in_c = jnp.logical_and(odd, jnp.logical_or(relaxed(group), relaxed((group + 1) % groups)))
+    copies = []
+    for side, (own, usual, other, moved, start) in enumerate(
+        (
+            (first_ref, got_a, got_b, left_in_b, 0),
+            (last_ref, got_b, got_c, right_in_c, out_ref.shape[1] - EDGE),
+        )
+    ):
+        for flag, got in ((jnp.logical_not(moved), usual), (moved, other)):
+
+            @pl.when(flag)
+            def _(side=side, own=own, got=got):
+                buf[side] = (own[...] + got[...].astype(F32)).astype(BF16)
+
+        copies.append(pltpu.make_async_copy(buf.at[side], out_ref.at[:, pl.ds(start, EDGE)], sems.at[side]))
+        copies[-1].start()
+    for copy in copies:
+        copy.wait()
 
 
 def off_chip(value):
@@ -141,14 +176,22 @@
     width = state.shape[2]
     cols = state.reshape(ROWS, width)
     groups = lax.axis_size(AXES)
-    up = [(i, (i + 1) % groups) for i in range(groups)]
-    down = [(b, a) for a, b in up]
+    pairs = {"a": [], "b": [], "c": []}
+    for i in range(groups):
+        nxt = (i + 1) % groups
+        if i % 2:
+            pairs["a"].append((i, nxt))
+            pairs["c" if relaxed(i) | relaxed(nxt) else "b"].append((nxt, i))
+        else:
+            pairs["b" if relaxed(i) else "a"].append((i, nxt))
+            pairs["b"].append((nxt, i))
     frac = sun_frac.reshape(width // EDGE, EDGE)
     chunks = (width - 2 * EDGE) // CHUNK
 
-    send_first, send_last, raw_first, raw_last, mix, pair, bias, frac, land, inner = pl.pallas_call(
+    send_first, send_last, send_mixed, raw_first, raw_last, mix, pair, bias, frac, land, inner = pl.pallas_call(
         edges_kernel,
         out_shape=(
+            pltpu.VMEM((ROWS, EDGE), BF16),
             pltpu.VMEM((ROWS, EDGE), BF16),
             pltpu.VMEM((ROWS, EDGE), BF16),
             pltpu.VMEM((ROWS, EDGE), F32),
@@ -161,7 +204,7 @@
             pltpu.VMEM((ROWS, width - 2 * EDGE), BF16),
         ),
         in_specs=[HBM] * 8,
-        out_specs=[VMEM] * 10,
+        out_specs=[VMEM] * 11,
         scratch_shapes=[
             pltpu.VMEM((ROWS, 2 * EDGE), BF16),
             pltpu.VMEM((width // EDGE, EDGE), BF16),
@@ -173,8 +216,9 @@
         name="edges",
     )(*map(off_chip, (land_count, cols, frac, mixing, canopy_sun, canopy_shade, bias_sun.reshape(1, HALF), bias_shade.reshape(1, HALF))))
 
-    from_left = lax.ppermute(send_last, AXES, up)
-    from_right = lax.ppermute(send_first, AXES, down)
+    got_a = lax.ppermute(send_last, AXES, pairs["a"])
+    got_b = lax.ppermute(send_mixed, AXES, pairs["b"])
+    got_c = lax.ppermute(send_first, AXES, pairs["c"])
 
     out = pl.pallas_call(
         inner_kernel,
@@ -186,23 +230,16 @@
         name="inner",
     )(on_chip(inner), on_chip(frac), on_chip(land), on_chip(mix), on_chip(pair), on_chip(bias))
 
-    def joined(out, got, own, block, name):
-        def body(*refs):
-            join_kernel(block, *refs)
-
-        return pl.pallas_call(
-            body,
-            out_shape=jax.ShapeDtypeStruct((ROWS, width), BF16),
-            in_specs=[VMEM, VMEM, HBM],
-            out_specs=HBM,
-            scratch_shapes=[pltpu.VMEM((ROWS, EDGE), BF16), pltpu.SemaphoreType.DMA],
-            input_output_aliases={2: 0},
-            compiler_params=pltpu.CompilerParams(vmem_limit_bytes=VMEM_BYTES),
-            name=name,
-        )(on_chip(got), on_chip(own), out)
-
-    out = joined(out, from_left, raw_first, 0, "join_left")
-    out = joined(out, from_right, raw_last, width // EDGE - 1, "join_right")
+    out = pl.pallas_call(
+        join_kernel,
+        out_shape=jax.ShapeDtypeStruct((ROWS, width), BF16),
+        in_specs=[*[VMEM] * 5, HBM],
+        out_specs=HBM,
+        scratch_shapes=[pltpu.VMEM((2, ROWS, EDGE), BF16), pltpu.SemaphoreType.DMA((2,))],
+        input_output_aliases={5: 0},
+        compiler_params=pltpu.CompilerParams(vmem_limit_bytes=VMEM_BYTES),
+        name="join",
+    )(*map(on_chip, (got_a, got_b, got_c, raw_first, raw_last)), out)
     return out.reshape(state.shape)
 
 

time: 26.9 us -> 25.8 us (0.959)
  the two profiles are of different devices: /device:TPU:384 before, /device:TPU:328 now
where the time goes in v2:
time: 25.8 us; the launch traced here: 25.6 us
  starting transfers between devices  11.3 us (44%)
  Pallas kernels  8.09 us (31%)
  waiting for transfers between devices  6.15 us (24%)
    ppermute x1, starting transfers between devices, per_device(): got_a = lax.ppermute(send_last, AXES, pairs['a'])  6.83 us
    ppermute x1, waiting for transfers between devices, per_device(): got_a = lax.ppermute(send_last, AXES, pairs['a'])  6.15 us
    pallas_call x1, Pallas kernels, per_device(): pl.pallas_call(inner_kernel, out_shape=jax.ShapeDtypeStruct((ROWS, width)...  5.16 us
    ppermute x1, starting transfers between devices, per_device(): got_b = lax.ppermute(send_mixed, AXES, pairs['b'])  3.85 us
    pallas_call x1, Pallas kernels, per_device(): pl.pallas_call(edges_kernel, out_shape=(pltpu.VMEM((ROWS, EDGE), BF16), p...  2.19 us
    pallas_call x1, Pallas kernels, per_device(): pl.pallas_call(join_kernel, out_shape=jax.ShapeDtypeStruct((ROWS, width),...  0.74 us
    ppermute x1, starting transfers between devices, per_device(): got_c = lax.ppermute(send_first, AXES, pairs['c'])  0.67 us
  transfers between devices with their start and end apart: 3, of which 1 were waited for; matrix products, arithmetic and copies ran while one was open for 0% of the time, Pallas kernels for 20%

profile of v2, /device:TPU:328, one launch (start us, length us, event | category | flops | bytes accessed | tf_op | source)
XLA Modules:
  0.0 25.6 jit_solution(12646859752650675334)
XLA Ops:
  0.0 2.2 %edges.1 = (bf16[512,128]{1,0:T(8,128)(2,1)S(1)}, bf16[512,128]{1,0:T(8,128)(2,1)S(1)}, bf16[512,128]{1,0:T(8,128)(2,1)S(1)}, f32[512,128]{1,0:T(8,128)S(1)}, f3...) custom-call(s32[768]{0:T(1024)} %land_ref.1, ...), custom_call_target="tpu_custom_call" | custom-call | tf_op jit(solution)/shard_map/edges/pallas_call | solution.py:191
  2.2 6.8 %collective-permute-start = (bf16[512,128]{1,0:T(8,128)(2,1)S(1)}, bf16[512,128]{1,0:T(8,128)(2,1)S(1)}, u32[]{:S(2)}, u32[]{:S(2)}) collective-permute-start(bf16[512,128]{1,0:T(8,128)(2,1)S(1)} %get-tuple-element.16), channel_id=1, source_target_pairs={{0,1},{1,2},{2,3},{3,4},{4,5},{5,6},{6,7},{7,8},{8,9},{9,10},{10,1... | collective-permute-start | bytes 393224 | tf_op jit(solution)/shard_map/ppermute | solution.py:219
  9.0 3.9 %collective-permute-start.1 = (bf16[512,128]{1,0:T(8,128)(2,1)S(1)}, bf16[512,128]{1,0:T(8,128)(2,1)S(1)}, u32[]{:S(2)}, u32[]{:S(2)}) collective-permute-start(bf16[512,128]{1,0:T(8,128)(2,1)S(1)} %get-tuple-element.17), channel_id=1, source_target_pairs={{1,0},{2,1},{3,2},{4,3},{5,4},{6,5},{7,6},{8,7},{9,8},{10,9},{11,1... | collective-permute-start | bytes 393224 | tf_op jit(solution)/shard_map/ppermute | solution.py:220
  12.9 0.7 %collective-permute-start.2 = (bf16[512,128]{1,0:T(8,128)(2,1)S(1)}, bf16[512,128]{1,0:T(8,128)(2,1)S(1)}, u32[]{:S(2)}, u32[]{:S(2)}) collective-permute-start(bf16[512,128]{1,0:T(8,128)(2,1)S(1)} %get-tuple-element.18), channel_id=1, source_target_pairs={{64,63},{66,65},{68,67},{70,69},{72,71},{128,127},{130,129},{132,1... | collective-permute-start | bytes 393224 | tf_op jit(solution)/shard_map/ppermute | solution.py:221
  13.6 5.2 %inner.1.all_ref = bf16[512,2048]{1,0:T(8,128)(2,1)} custom-call(bf16[512,1792]{1,0:T(8,128)(2,1)S(1)} %get-tuple-element.21.cols_ref, f32[16,128]{1,0:T(8,128)S(1)} %get-tuple-element.22.frac_ref, f32[16,128]{1,0:T(8,128)S(1)} %get-tuple-element.23.land_ref, bf16[512,512]{1,0:T(8,128)(2,1)S(1)} %get-tuple-element.24.mixing_ref, ...), custom_call_target="tpu_custom_call" | custom-call | tf_op jit(solution)/shard_map/inner/pallas_call | solution.py:223
  18.7 6.1 %collective-permute-done.got_a = bf16[512,128]{1,0:T(8,128)(2,1)S(1)} collective-permute-done((bf16[512,128]{1,0:T(8,128)(2,1)S(1)}, bf16[512,128]{1,0:T(8,128)(2,1)S(1)}, u32[]{:S(2)}, u32[]{:S(2)}) %collective-permute-start) | collective-permute-done | bytes 131104 | tf_op jit(solution)/shard_map/ppermute | solution.py:219
  24.9 0.0 collective-permute-done.1.got_b
  24.9 0.0 collective-permute-done.2.got_c
  24.9 0.7 %join.1 = bf16[512,2048]{1,0:T(8,128)(2,1)} custom-call(bf16[512,128]{1,0:T(8,128)(2,1)S(1)} %collective-permute-done.got_a, bf16[512,128]{1,0:T(8,128)(2,1)S(1)} %collective-permute-done.1.got_b, bf16[512,128]{1,0:T(8,128)(2,1)S(1)} %collective-permute-done.2.got_c, f32[512,128]{1,0:T(8,128)S(1)} %get-tuple-element.19.first_ref, ...), custom_call_target="tpu_custom_call", output_to_operand_aliasing={{}: (5, {})} | custom-call | tf_op jit(solution)/shard_map/join/pallas_call | solution.py:233
Async XLA Ops:
  2.2 22.7 %collective-permute-start = (bf16[512,128]{1,0:T(8,128)(2,1)S(1)}, bf16[512,128]{1,0:T(8,128)(2,1)S(1)}, u32[]{:S(2)}, u32[]{:S(2)}) collective-permute-start(bf16[512,128]{1,0:T(8,128)(2,1)S(1)} %get-tuple-element.16), channel_id=1, source_target_pairs={{0,1},{1,2},{2,3},{3,4},{4,5},{5,6},{6,7},{7,8},{8,9},{9,10},{10,1... | collective-permute-start | bytes 393224 | tf_op jit(solution)/shard_map/ppermute | solution.py:219
  9.0 15.9 %collective-permute-start.1 = (bf16[512,128]{1,0:T(8,128)(2,1)S(1)}, bf16[512,128]{1,0:T(8,128)(2,1)S(1)}, u32[]{:S(2)}, u32[]{:S(2)}) collective-permute-start(bf16[512,128]{1,0:T(8,128)(2,1)S(1)} %get-tuple-element.17), channel_id=1, source_target_pairs={{1,0},{2,1},{3,2},{4,3},{5,4},{6,5},{7,6},{8,7},{9,8},{10,9},{11,1... | collective-permute-start | bytes 393224 | tf_op jit(solution)/shard_map/ppermute | solution.py:220
  12.9 12.0 %collective-permute-start.2 = (bf16[512,128]{1,0:T(8,128)(2,1)S(1)}, bf16[512,128]{1,0:T(8,128)(2,1)S(1)}, u32[]{:S(2)}, u32[]{:S(2)}) collective-permute-start(bf16[512,128]{1,0:T(8,128)(2,1)S(1)} %get-tuple-element.18), channel_id=1, source_target_pairs={{64,63},{66,65},{68,67},{70,69},{72,71},{128,127},{130,129},{132,1... | collective-permute-start | bytes 393224 | tf_op jit(solution)/shard_map/ppermute | solution.py:221

commit v3 on v2

--- a/solution.py
+++ b/solution.py
@@ -53,6 +53,10 @@
 def relaxed(group):
     nsub = lax.axis_size("sub")
     return ((group // nsub) % 8 == 0) & (group >= nsub)
+
+
+def patient(group):
+    return (group // (2 * lax.axis_size("sub"))) % 4 >= 2
 
 
 def lanes():
@@ -141,6 +145,7 @@
     odd = group % 2 == 1
     left_in_b = jnp.logical_and(odd, relaxed(group))
     right_in_c = jnp.logical_and(odd, jnp.logical_or(relaxed(group), relaxed((group + 1) % groups)))
+    right_in_c = jnp.logical_or(right_in_c, patient(group))
     copies = []
     for side, (own, usual, other, moved, start) in enumerate(
         (
@@ -181,10 +186,10 @@
         nxt = (i + 1) % groups
         if i % 2:
             pairs["a"].append((i, nxt))
-            pairs["c" if relaxed(i) | relaxed(nxt) else "b"].append((nxt, i))
+            pairs["c" if relaxed(i) | relaxed(nxt) | patient(i) else "b"].append((nxt, i))
         else:
             pairs["b" if relaxed(i) else "a"].append((i, nxt))
-            pairs["b"].append((nxt, i))
+            pairs["c" if patient(i) else "b"].append((nxt, i))
     frac = sun_frac.reshape(width // EDGE, EDGE)
     chunks = (width - 2 * EDGE) // CHUNK
 

time: 25.8 us -> 26 us (level)
  the two profiles are of different devices: /device:TPU:328 before, /device:TPU:16 now
where the time goes in v3:
time: 26 us; the launch traced here: 25.8 us
  starting transfers between devices  12 us (46%)
  Pallas kernels  8.08 us (31%)
  waiting for transfers between devices  5.69 us (22%)
    ppermute x1, starting transfers between devices, per_device(): got_a = lax.ppermute(send_last, AXES, pairs['a'])  5.94 us
    ppermute x1, waiting for transfers between devices, per_device(): got_c = lax.ppermute(send_first, AXES, pairs['c'])  5.69 us
    pallas_call x1, Pallas kernels, per_device(): pl.pallas_call(inner_kernel, out_shape=jax.ShapeDtypeStruct((ROWS, width)...  5.16 us
    ppermute x1, starting transfers between devices, per_device(): got_b = lax.ppermute(send_mixed, AXES, pairs['b'])  4.75 us
    pallas_call x1, Pallas kernels, per_device(): pl.pallas_call(edges_kernel, out_shape=(pltpu.VMEM((ROWS, EDGE), BF16), p...  2.19 us
    ppermute x1, starting transfers between devices, per_device(): got_c = lax.ppermute(send_first, AXES, pairs['c'])  1.29 us
    pallas_call x1, Pallas kernels, per_device(): pl.pallas_call(join_kernel, out_shape=jax.ShapeDtypeStruct((ROWS, width),...  0.74 us
  transfers between devices with their start and end apart: 3, of which 1 were waited for; matrix products, arithmetic and copies ran while one was open for 0% of the time, Pallas kernels for 20%

profile of v3, /device:TPU:16, one launch (start us, length us, event | category | flops | bytes accessed | tf_op | source)
XLA Modules:
  0.0 25.8 jit_solution(11731547263903889602)
XLA Ops:
  0.0 2.2 %edges.1 = (bf16[512,128]{1,0:T(8,128)(2,1)S(1)}, bf16[512,128]{1,0:T(8,128)(2,1)S(1)}, bf16[512,128]{1,0:T(8,128)(2,1)S(1)}, f32[512,128]{1,0:T(8,128)S(1)}, f3...) custom-call(s32[768]{0:T(1024)} %land_ref.1, ...), custom_call_target="tpu_custom_call" | custom-call | tf_op jit(solution)/shard_map/edges/pallas_call | solution.py:196
  2.2 5.9 %collective-permute-start = (bf16[512,128]{1,0:T(8,128)(2,1)S(1)}, bf16[512,128]{1,0:T(8,128)(2,1)S(1)}, u32[]{:S(2)}, u32[]{:S(2)}) collective-permute-start(bf16[512,128]{1,0:T(8,128)(2,1)S(1)} %get-tuple-element.16), channel_id=1, source_target_pairs={{0,1},{1,2},{2,3},{3,4},{4,5},{5,6},{6,7},{7,8},{8,9},{9,10},{10,1... | collective-permute-start | bytes 393224 | tf_op jit(solution)/shard_map/ppermute | solution.py:224
  8.1 4.7 %collective-permute-start.1 = (bf16[512,128]{1,0:T(8,128)(2,1)S(1)}, bf16[512,128]{1,0:T(8,128)(2,1)S(1)}, u32[]{:S(2)}, u32[]{:S(2)}) collective-permute-start(bf16[512,128]{1,0:T(8,128)(2,1)S(1)} %get-tuple-element.17), channel_id=1, source_target_pairs={{1,0},{2,1},{3,2},{4,3},{5,4},{6,5},{7,6},{8,7},{9,8},{10,9},{11,1... | collective-permute-start | bytes 393224 | tf_op jit(solution)/shard_map/ppermute | solution.py:225
  12.9 1.3 %collective-permute-start.2 = (bf16[512,128]{1,0:T(8,128)(2,1)S(1)}, bf16[512,128]{1,0:T(8,128)(2,1)S(1)}, u32[]{:S(2)}, u32[]{:S(2)}) collective-permute-start(bf16[512,128]{1,0:T(8,128)(2,1)S(1)} %get-tuple-element.18), channel_id=1, source_target_pairs={{33,32},{34,33},{35,34},{36,35},{37,36},{38,37},{39,38},{40,39},{4... | collective-permute-start | bytes 393224 | tf_op jit(solution)/shard_map/ppermute | solution.py:226
  14.2 5.2 %inner.1.all_ref = bf16[512,2048]{1,0:T(8,128)(2,1)} custom-call(bf16[512,1792]{1,0:T(8,128)(2,1)S(1)} %get-tuple-element.21.cols_ref, f32[16,128]{1,0:T(8,128)S(1)} %get-tuple-element.22.frac_ref, f32[16,128]{1,0:T(8,128)S(1)} %get-tuple-element.23.land_ref, bf16[512,512]{1,0:T(8,128)(2,1)S(1)} %get-tuple-element.24.mixing_ref, ...), custom_call_target="tpu_custom_call" | custom-call | tf_op jit(solution)/shard_map/inner/pallas_call | solution.py:228
  19.4 0.0 collective-permute-done.got_a
  19.4 0.0 collective-permute-done.1.got_b
  19.4 5.7 %collective-permute-done.2.got_c = bf16[512,128]{1,0:T(8,128)(2,1)S(1)} collective-permute-done((bf16[512,128]{1,0:T(8,128)(2,1)S(1)}, bf16[512,128]{1,0:T(8,128)(2,1)S(1)}, u32[]{:S(2)}, u32[]{:S(2)}) %collective-permute-start.2) | collective-permute-done | bytes 131104 | tf_op jit(solution)/shard_map/ppermute | solution.py:226
  25.1 0.7 %join.1 = bf16[512,2048]{1,0:T(8,128)(2,1)} custom-call(bf16[512,128]{1,0:T(8,128)(2,1)S(1)} %collective-permute-done.got_a, bf16[512,128]{1,0:T(8,128)(2,1)S(1)} %collective-permute-done.1.got_b, bf16[512,128]{1,0:T(8,128)(2,1)S(1)} %collective-permute-done.2.got_c, f32[512,128]{1,0:T(8,128)S(1)} %get-tuple-element.19.first_ref, ...), custom_call_target="tpu_custom_call", output_to_operand_aliasing={{}: (5, {})} | custom-call | tf_op jit(solution)/shard_map/join/pallas_call | solution.py:238
Async XLA Ops:
  2.2 17.2 %collective-permute-start = (bf16[512,128]{1,0:T(8,128)(2,1)S(1)}, bf16[512,128]{1,0:T(8,128)(2,1)S(1)}, u32[]{:S(2)}, u32[]{:S(2)}) collective-permute-start(bf16[512,128]{1,0:T(8,128)(2,1)S(1)} %get-tuple-element.16), channel_id=1, source_target_pairs={{0,1},{1,2},{2,3},{3,4},{4,5},{5,6},{6,7},{7,8},{8,9},{9,10},{10,1... | collective-permute-start | bytes 393224 | tf_op jit(solution)/shard_map/ppermute | solution.py:224
  8.1 11.2 %collective-permute-start.1 = (bf16[512,128]{1,0:T(8,128)(2,1)S(1)}, bf16[512,128]{1,0:T(8,128)(2,1)S(1)}, u32[]{:S(2)}, u32[]{:S(2)}) collective-permute-start(bf16[512,128]{1,0:T(8,128)(2,1)S(1)} %get-tuple-element.17), channel_id=1, source_target_pairs={{1,0},{2,1},{3,2},{4,3},{5,4},{6,5},{7,6},{8,7},{9,8},{10,9},{11,1... | collective-permute-start | bytes 393224 | tf_op jit(solution)/shard_map/ppermute | solution.py:225
  12.9 12.2 %collective-permute-start.2 = (bf16[512,128]{1,0:T(8,128)(2,1)S(1)}, bf16[512,128]{1,0:T(8,128)(2,1)S(1)}, u32[]{:S(2)}, u32[]{:S(2)}) collective-permute-start(bf16[512,128]{1,0:T(8,128)(2,1)S(1)} %get-tuple-element.18), channel_id=1, source_target_pairs={{33,32},{34,33},{35,34},{36,35},{37,36},{38,37},{39,38},{40,39},{4... | collective-permute-start | bytes 393224 | tf_op jit(solution)/shard_map/ppermute | solution.py:226

commit v4 on v3

--- a/solution.py
+++ b/solution.py
@@ -56,7 +56,7 @@
 
 
 def patient(group):
-    return (group // (2 * lax.axis_size("sub"))) % 4 >= 2
+    return (group // (2 * lax.axis_size("sub"))) % 4 == 3
 
 
 def lanes():

time: 26 us -> 25.6 us (0.985)
  the two profiles are of different devices: /device:TPU:16 before, /device:TPU:4 now
where the time goes in v4:
time: 25.6 us; the launch traced here: 25.4 us
  starting transfers between devices  11.3 us (44%)
  Pallas kernels  8.08 us (32%)
  waiting for transfers between devices  5.96 us (23%)
    ppermute x1, starting transfers between devices, per_device(): got_a = lax.ppermute(send_last, AXES, pairs['a'])  7.74 us
    ppermute x1, waiting for transfers between devices, per_device(): got_b = lax.ppermute(send_mixed, AXES, pairs['b'])  5.96 us
    pallas_call x1, Pallas kernels, per_device(): pl.pallas_call(inner_kernel, out_shape=jax.ShapeDtypeStruct((ROWS, width)...  5.16 us
    ppermute x1, starting transfers between devices, per_device(): got_b = lax.ppermute(send_mixed, AXES, pairs['b'])  2.91 us
    pallas_call x1, Pallas kernels, per_device(): pl.pallas_call(edges_kernel, out_shape=(pltpu.VMEM((ROWS, EDGE), BF16), p...  2.18 us
    pallas_call x1, Pallas kernels, per_device(): pl.pallas_call(join_kernel, out_shape=jax.ShapeDtypeStruct((ROWS, width),...  0.74 us
    ppermute x1, starting transfers between devices, per_device(): got_c = lax.ppermute(send_first, AXES, pairs['c'])  0.67 us
  transfers between devices with their start and end apart: 3, of which 1 were waited for; matrix products, arithmetic and copies ran while one was open for 0% of the time, Pallas kernels for 20%

profile of v4, /device:TPU:4, one launch (start us, length us, event | category | flops | bytes accessed | tf_op | source)
XLA Modules:
  0.0 25.4 jit_solution(16708069253413818714)
XLA Ops:
  0.0 2.2 %edges.1 = (bf16[512,128]{1,0:T(8,128)(2,1)S(1)}, bf16[512,128]{1,0:T(8,128)(2,1)S(1)}, bf16[512,128]{1,0:T(8,128)(2,1)S(1)}, f32[512,128]{1,0:T(8,128)S(1)}, f3...) custom-call(s32[768]{0:T(1024)} %land_ref.1, ...), custom_call_target="tpu_custom_call" | custom-call | tf_op jit(solution)/shard_map/edges/pallas_call | solution.py:196
  2.2 7.7 %collective-permute-start = (bf16[512,128]{1,0:T(8,128)(2,1)S(1)}, bf16[512,128]{1,0:T(8,128)(2,1)S(1)}, u32[]{:S(2)}, u32[]{:S(2)}) collective-permute-start(bf16[512,128]{1,0:T(8,128)(2,1)S(1)} %get-tuple-element.16), channel_id=1, source_target_pairs={{0,1},{1,2},{2,3},{3,4},{4,5},{5,6},{6,7},{7,8},{8,9},{9,10},{10,1... | collective-permute-start | bytes 393224 | tf_op jit(solution)/shard_map/ppermute | solution.py:224
  9.9 2.9 %collective-permute-start.1 = (bf16[512,128]{1,0:T(8,128)(2,1)S(1)}, bf16[512,128]{1,0:T(8,128)(2,1)S(1)}, u32[]{:S(2)}, u32[]{:S(2)}) collective-permute-start(bf16[512,128]{1,0:T(8,128)(2,1)S(1)} %get-tuple-element.17), channel_id=1, source_target_pairs={{1,0},{2,1},{3,2},{4,3},{5,4},{6,5},{7,6},{8,7},{9,8},{10,9},{11,1... | collective-permute-start | bytes 393224 | tf_op jit(solution)/shard_map/ppermute | solution.py:225
  12.9 0.7 %collective-permute-start.2 = (bf16[512,128]{1,0:T(8,128)(2,1)S(1)}, bf16[512,128]{1,0:T(8,128)(2,1)S(1)}, u32[]{:S(2)}, u32[]{:S(2)}) collective-permute-start(bf16[512,128]{1,0:T(8,128)(2,1)S(1)} %get-tuple-element.18), channel_id=1, source_target_pairs={{49,48},{50,49},{51,50},{52,51},{53,52},{54,53},{55,54},{56,55},{5... | collective-permute-start | bytes 393224 | tf_op jit(solution)/shard_map/ppermute | solution.py:226
  13.5 5.2 %inner.1.all_ref = bf16[512,2048]{1,0:T(8,128)(2,1)} custom-call(bf16[512,1792]{1,0:T(8,128)(2,1)S(1)} %get-tuple-element.21.cols_ref, f32[16,128]{1,0:T(8,128)S(1)} %get-tuple-element.22.frac_ref, f32[16,128]{1,0:T(8,128)S(1)} %get-tuple-element.23.land_ref, bf16[512,512]{1,0:T(8,128)(2,1)S(1)} %get-tuple-element.24.mixing_ref, ...), custom_call_target="tpu_custom_call" | custom-call | tf_op jit(solution)/shard_map/inner/pallas_call | solution.py:228
  18.7 0.0 collective-permute-done.got_a
  18.7 6.0 %collective-permute-done.1.got_b = bf16[512,128]{1,0:T(8,128)(2,1)S(1)} collective-permute-done((bf16[512,128]{1,0:T(8,128)(2,1)S(1)}, bf16[512,128]{1,0:T(8,128)(2,1)S(1)}, u32[]{:S(2)}, u32[]{:S(2)}) %collective-permute-start.1) | collective-permute-done | bytes 131104 | tf_op jit(solution)/shard_map/ppermute | solution.py:225
  24.7 0.0 collective-permute-done.2.got_c
  24.7 0.7 %join.1 = bf16[512,2048]{1,0:T(8,128)(2,1)} custom-call(bf16[512,128]{1,0:T(8,128)(2,1)S(1)} %collective-permute-done.got_a, bf16[512,128]{1,0:T(8,128)(2,1)S(1)} %collective-permute-done.1.got_b, bf16[512,128]{1,0:T(8,128)(2,1)S(1)} %collective-permute-done.2.got_c, f32[512,128]{1,0:T(8,128)S(1)} %get-tuple-element.19.first_ref, ...), custom_call_target="tpu_custom_call", output_to_operand_aliasing={{}: (5, {})} | custom-call | tf_op jit(solution)/shard_map/join/pallas_call | solution.py:238
Async XLA Ops:
  2.2 16.5 %collective-permute-start = (bf16[512,128]{1,0:T(8,128)(2,1)S(1)}, bf16[512,128]{1,0:T(8,128)(2,1)S(1)}, u32[]{:S(2)}, u32[]{:S(2)}) collective-permute-start(bf16[512,128]{1,0:T(8,128)(2,1)S(1)} %get-tuple-element.16), channel_id=1, source_target_pairs={{0,1},{1,2},{2,3},{3,4},{4,5},{5,6},{6,7},{7,8},{8,9},{9,10},{10,1... | collective-permute-start | bytes 393224 | tf_op jit(solution)/shard_map/ppermute | solution.py:224
  9.9 14.7 %collective-permute-start.1 = (bf16[512,128]{1,0:T(8,128)(2,1)S(1)}, bf16[512,128]{1,0:T(8,128)(2,1)S(1)}, u32[]{:S(2)}, u32[]{:S(2)}) collective-permute-start(bf16[512,128]{1,0:T(8,128)(2,1)S(1)} %get-tuple-element.17), channel_id=1, source_target_pairs={{1,0},{2,1},{3,2},{4,3},{5,4},{6,5},{7,6},{8,7},{9,8},{10,9},{11,1... | collective-permute-start | bytes 393224 | tf_op jit(solution)/shard_map/ppermute | solution.py:225
  12.9 11.8 %collective-permute-start.2 = (bf16[512,128]{1,0:T(8,128)(2,1)S(1)}, bf16[512,128]{1,0:T(8,128)(2,1)S(1)}, u32[]{:S(2)}, u32[]{:S(2)}) collective-permute-start(bf16[512,128]{1,0:T(8,128)(2,1)S(1)} %get-tuple-element.18), channel_id=1, source_target_pairs={{49,48},{50,49},{51,50},{52,51},{53,52},{54,53},{55,54},{56,55},{5... | collective-permute-start | bytes 393224 | tf_op jit(solution)/shard_map/ppermute | solution.py:226
